TPU v7x, 128 devices: a whole 4x4x4 slice. The times are simulated.
128 devices in a mesh: gx: 8 (over x_hi, z), gy: 4 (over y), gz: 4 (over x_lo, core).
Axes of the slice: x: 4 (x_hi: 2, x_lo: 2; x = x_hi * 2 + x_lo), y: 4, z: 4, core: 2. Of those that a mesh axis runs over, the one named last changes fastest.
Arguments:
- panels: bfloat16 [12288, 8192], P(('gx', 'gy'), 'gz'), may hold values from -0.75 to 0.75
- sizes: int32 [8], replicated, may hold values from 1 to 1024
- front: float32 [12288, 12288], P(('gx', 'gz'), 'gy'), may hold values from -6 to 6
Outputs:
- updated: float32 [12288, 12288], P(('gx', 'gz'), 'gy')
All inputs are finite; a program needn't handle non-finite values.
Results may differ from a plain program's by a relative error of at most 0.0003.
Values may be sent and summed in bfloat16 or wider, within the bound.
A program may use at most 128 MiB of HBM per device.

v0:
```python
import jax
import jax.numpy as jnp
from jax import lax
from jax.sharding import Mesh
from jax.sharding import PartitionSpec as P

WIDTH = 1024
GZ = ("gz_0", "gz_1")
GX_GZ = ("gx", "gz_0", "gz_1")


def sum_in_order(blocks, axes, sequence):
    inside = blocks.shape[1:]
    blocks = blocks.reshape(*(lax.axis_size(a) for a in axes), *inside)
    blocks = jnp.moveaxis(blocks, sequence, range(len(axes))).reshape(-1, *inside)
    for k in sequence:
        blocks = lax.psum_scatter(blocks, axes[k], scatter_dimension=0, tiled=True)
    return blocks[0]


def split_up(value, dim, size):
    shape = value.shape
    blocks = value.reshape(*shape[:dim], size, shape[dim] // size, *shape[dim + 1 :])
    return jnp.moveaxis(blocks, dim, 0)


def scatter_axes(value, axes, sequence, dim):
    size = lax.axis_size(axes)
    return sum_in_order(split_up(value, dim, size), axes, sequence)


def shards(panels, sizes, front):
    panel_count = panels.shape[1] // WIDTH
    first = lax.axis_index(GZ) * panel_count
    limits = lax.dynamic_slice_in_dim(sizes, first, panel_count, 0)
    column = jnp.arange(WIDTH, dtype=jnp.int32)
    live = (column[None, :] < limits[:, None]).reshape(panel_count * WIDTH).astype(jnp.bfloat16)
    row_part = lax.all_gather(panels, "gy", axis=0, tiled=True)
    column_part = lax.all_gather(panels, "gx", axis=0, tiled=True)
    masked = row_part * live[None, :]
    summed = scatter_axes(
        -lax.dot_general(
            masked, column_part, (((1,), (1,)), ((), ())), preferred_element_type=jnp.float32
        ),
        GZ,
        (1, 0),
        0,
    )
    return front + summed


def solution(mesh):
    split = Mesh(
        mesh.devices.reshape(mesh.shape["gx"], mesh.shape["gy"], 2, 2), ("gx", "gy", "gz_0", "gz_1")
    )
    placed = (P(("gx", "gy"), GZ), P(), P(GX_GZ, "gy"))
    return jax.shard_map(
        shards, mesh=split, in_specs=placed, out_specs=P(GX_GZ, "gy"), check_vma=False
    )
```

profile of v0, /device:TPU:1, one launch (start us, length us, event | category | flops | bytes accessed | tf_op | source)
XLA Modules:
  0.0 414.5 jit_solution(5488755686385768562)
XLA Ops:
  6.5 0.0 all-gather.3.cloned.1.call-start
  6.5 0.7 all-gather.3.cloned.1.call-update
  7.3 0.0 all-gather.5.cloned.1.call-start
  7.3 0.7 all-gather.5.cloned.1.call-update
  8.0 0.0 reduce-scatter.3.cloned.1.call-start
  8.1 0.7 dynamic_slice.3
  8.8 0.1 fusion.2
  8.9 68.8 %all-gather.3.cloned.1.call-done = bf16[1536,2048]{1,0:T(8,128)(2,1)} async-done(((bf16[384,2048]{1,0:T(8,128)(2,1)}), bf16[1536,2048]{1,0:T(8,128)(2,1)}) %all-gather.3.cloned.1.call-update) | async-done | bytes 6291472 | tf_op jit(solution)/shard_map/all_gather | solution.py:38
  77.7 147.0 %all-gather.5.cloned.1.call-done = bf16[3072,2048]{1,0:T(8,128)(2,1)} async-done(((bf16[384,2048]{1,0:T(8,128)(2,1)}), bf16[3072,2048]{1,0:T(8,128)(2,1)}) %all-gather.5.cloned.1.call-update) | async-done | bytes 12582928 | tf_op jit(solution)/shard_map/all_gather | solution.py:39
  224.7 24.8 %convolution_negate_fusion = f32[1536,3072]{1,0:T(8,128)S(1)} fusion(bf16[3072,2048]{1,0:T(8,128)(2,1)} %all-gather.5.cloned.1.call-done, bf16[1536,2048]{1,0:T(8,128)(2,1)} %all-gather.3.cloned.1.call-done, bf16[2048]{0:T(1024)(128)(2,1)S(1)} %bitcast.14), kind=kOutput, calls=%fused_computation | convolution fusion | flops 19335217152 | bytes 37752832 | tf_op jit(solution)/shard_map/dot_general | solution.py:42
  249.5 6.8 %copy.4 = f32[2,2,384,3072]{3,2,1,0:T(8,128)} copy(f32[2,2,384,3072]{3,2,0,1:T(8,128)S(1)} %bitcast.13) | data formatting | bytes 37748736 | tf_op jit(solution)/shard_map/transpose | solution.py:15
  256.3 0.0 reduce-scatter.3.cloned.1.call-update
  256.3 0.0 reduce-scatter.5.cloned.1.call-start
  256.4 28.2 %reduce-scatter.3.cloned.1.call-done = f32[2,384,3072]{2,1,0:T(8,128)} async-done(((f32[4,384,3072]{2,1,0:T(8,128)}), f32[2,384,3072]{2,1,0:T(8,128)}) %reduce-scatter.3.cloned.1.call-update) | async-done | bytes 9437200 | tf_op jit(solution)/shard_map/reduce_scatter | solution.py:17
  284.6 0.0 reduce-scatter.5.cloned.1.call-update
  284.6 116.4 %reduce-scatter.5.cloned.1.call-done = f32[1,384,3072]{2,1,0:T(8,128)} async-done(((f32[2,384,3072]{2,1,0:T(8,128)}), f32[1,384,3072]{2,1,0:T(8,128)}) %reduce-scatter.5.cloned.1.call-update) | async-done | bytes 4718608 | tf_op jit(solution)/shard_map/reduce_scatter | solution.py:17
  401.0 7.0 %bitcast_add_fusion = f32[384,3072]{1,0:T(8,128)} fusion(f32[384,3072]{1,0:T(8,128)} %param.5, f32[1,384,3072]{2,1,0:T(8,128)} %reduce-scatter.5.cloned.1.call-done), kind=kLoop, calls=%fused_computation.2 | loop fusion | flops 1179648 | bytes 14155776 | tf_op jit(solution)/shard_map/add | solution.py:49
  (1 shorter events, 0.0 us)
Async XLA Ops:
  6.5 71.2 %all-gather.3.cloned.1.call-start = ((), (), s32[]{:S(2)}) async-start(), calls=%async_computation.2 | async-start | bytes 7864320 | tf_op jit(solution)/shard_map/all_gather | solution.py:38
  7.3 217.4 %all-gather.5.cloned.1.call-start = ((), (), s32[]{:S(2)}) async-start(), calls=%async_computation.3 | async-start | bytes 14155776 | tf_op jit(solution)/shard_map/all_gather | solution.py:39
  8.0 276.5 %reduce-scatter.3.cloned.1.call-start = ((), (), s32[]{:S(2)}) async-start(), calls=%async_computation.4 | async-start | bytes 28311552 | tf_op jit(solution)/shard_map/reduce_scatter | solution.py:17
  256.3 144.6 %reduce-scatter.5.cloned.1.call-start = ((), (), s32[]{:S(2)}) async-start(), calls=%async_computation.5 | async-start | bytes 14155776 | tf_op jit(solution)/shard_map/reduce_scatter | solution.py:17
Sparse Core Ops, SparseCore 0:
  9.0 68.6 all-gather.2
  80.0 144.6 all-gather.4
  256.4 28.0 reduce-scatter.2
  286.8 114.0 reduce-scatter.4
where the time goes:
time: 415 us; the launch traced here: 414 us
  waiting for transfers between devices  362 us (87%)
  matrix products  24.8 us (6%)
  between operations  13.1 us (3%)
  local copies, waits for them, and re-layouts  7.55 us (2%)
  other arithmetic  7.05 us (2%)
    all_gather x1, waiting for transfers between devices, shards(): column_part = lax.all_gather(panels, 'gx', axis=0, tiled=True)  147 us
    reduce_scatter x2, waiting for transfers between devices, sum_in_order(): blocks = lax.psum_scatter(blocks, axes[k], scatter_dimension=0, tiled=True)  145 us
    all_gather x1, waiting for transfers between devices, shards(): row_part = lax.all_gather(panels, 'gy', axis=0, tiled=True)  68.8 us
    dot_general x1, matrix products, shards(): lax.dot_general(masked, column_part, (((1,), (1,)), ((), ())), preferred_...  24.8 us
  transfers between devices with their start and end apart: 4, of which 4 were waited for; matrix products, arithmetic and copies ran while one was open for 0% of the time, Pallas kernels for 0%

commit v1 on v0

v1 whole, which is shorter than its diff:
```python
import functools

import jax
import jax.numpy as jnp
from jax import lax
from jax.experimental import pallas as pl
from jax.experimental.pallas import tpu as pltpu
from jax.sharding import PartitionSpec as P

WIDTH = 1024
PIECE = 384
HALF = PIECE // 2
CHUNK = 512
MESH = pl.DeviceIdType.MESH
Q_AT = (0, 3, 1, 2)


def device(x, y, z, c):
    return (x // 2) * 4 + z, y, (x % 2) * 2 + c


def kernel(wide, p_ref, f_ref, o_ref, cols, rows, acc, s_send, s_recv, x_send, x_recv, y_send, y_recv, l_sem, f_sem, o_sem):
    gx, y, gz = lax.axis_index("gx"), lax.axis_index("gy"), lax.axis_index("gz")
    x_lo, c, z = gz // 2, gz % 2, gx % 4
    x = (gx // 4) * 2 + x_lo
    sign = 2 * c - 1

    def at(dx, dz):
        return ((x + dx) % 4) * 4 + (z + dz) % 4

    def slot(p, s):
        return at((1 - c) * p + c * s, c * p + (1 - c) * s)

    def along_p(d):
        return device((x + (1 - c) * d) % 4, y, (z + c * d) % 4, c)

    def along_s(d):
        return device((x + c * d) % 4, y, (z + (1 - c) * d) % 4, c)

    def along_y(d):
        return device(x, (y + 4 + d * sign) % 4, z, c)

    partner = device(x, y, z, 1 - c)
    mine = p_ref.at[:, pl.ds(0, wide)]
    whole, top, bottom = pl.ds(0, PIECE), pl.ds(0, HALF), pl.ds(HALF, HALF)

    def block(core, at_slot, part=whole):
        return cols.at[core, at_slot, part]

    def send(k, src, dst, to):
        return pltpu.make_async_remote_copy(src, dst, s_send.at[k], s_recv.at[k], device_id=to, device_id_type=MESH)

    def copy(k):
        if k < 2:
            return send(k, mine, block(c, slot(0, 0)), along_p(1 + 2 * k))
        if k < 4:
            ref = block(c, slot(3 if k == 2 else 1, 0), (top, bottom)[k - 2])
            return send(k, ref, ref, along_p(2 * k - 3))
        q, kind = k // 4 - 1, k % 4
        if kind < 2:
            here = block(c, slot(Q_AT[q], 0))
            return send(k, mine if q == 0 else here, here, along_s(1 + 2 * kind))
        ref = block(c, slot(Q_AT[q], 3 if kind == 2 else 1), (top, bottom)[kind - 2])
        return send(k, ref, ref, along_s(2 * kind - 3))

    def arrival(k):
        if k < 4:
            where = (slot(3, 0), slot(1, 0), slot(2, 0), slot(2, 0))[k]
        else:
            p = Q_AT[(k - 4) // 4]
            where = (slot(p, 3), slot(p, 1), slot(p, 2), slot(p, 2))[k % 4]
        part = (whole, whole, top, bottom)[k % 4]
        ref = block(c, where, part)
        return send(k, ref, ref, partner)

    def start(*ks):
        for k in ks:
            copy(k).start()

    def take(*ks):
        for k in ks:
            arrival(k).wait_recv()

    def swap(at_slot, src=None):
        src = block(c, at_slot) if src is None else src
        return pltpu.make_async_remote_copy(
            src, block(c, at_slot), x_send.at[at_slot], x_recv.at[at_slot], device_id=partner, device_id_type=MESH
        )

    def take_swap(at_slot):
        ref = block(1 - c, at_slot)
        pltpu.make_async_remote_copy(
            ref, ref, x_send.at[at_slot], x_recv.at[at_slot], device_id=partner, device_id_type=MESH
        ).wait_recv()

    place = ((y - gz) * sign + 8) % 4
    beside = x + 1 - 2 * x_lo

    def row_src(j):
        if j == 0:
            return mine
        return block(c if j % 2 == 0 else 1 - c, (beside if j >= 2 else x) * 4 + z)

    def row_copy(j, d):
        return pltpu.make_async_remote_copy(
            row_src(j), rows.at[j], y_send.at[j, 0 if d == 1 else 1], y_recv.at[j], device_id=along_y(d), device_id_type=MESH
        )

    def row_relay(j):
        return pltpu.make_async_remote_copy(
            rows.at[j], rows.at[j], y_send.at[j, 0], y_recv.at[j], device_id=along_y(1), device_id_type=MESH
        )

    def row_local(j):
        return pltpu.make_async_copy(row_src(j), rows.at[j], l_sem.at[j])

    def row_start(j):
        @pl.when(place == 0)
        def _():
            row_copy(j, 1).start()
            row_copy(j, -1).start()
            row_local(j).start()

    def row_forward(j):
        @pl.when(place == 1)
        def _():
            row_relay(j).wait_recv()
            row_relay(j).start()

    def row_take(j):
        @pl.when(place == 0)
        def _():
            row_local(j).wait()

        @pl.when(place >= 2)
        def _():
            row_relay(j).wait_recv()

    def front(a):
        return pltpu.make_async_copy(f_ref.at[:, pl.ds(a * PIECE, PIECE)], acc.at[a], f_sem.at[a])

    def result(a):
        a_at = pl.multiple_of(a * PIECE, PIECE)
        return pltpu.make_async_copy(acc.at[a], o_ref.at[:, pl.ds(a_at, PIECE)], o_sem.at[a])

    def multiply(dx, dz, other):
        xs, zs = (x + dx) % 4, (z + dz) % 4
        a = (xs // 2) * 4 + zs
        core = c + other * (1 - 2 * c)
        j = 2 * (dx % 2) + other

        @pl.loop(0, wide // CHUNK)
        def _(i):
            at_k = pl.ds(pl.multiple_of(i * CHUNK, CHUNK), CHUNK)
            acc[a] = acc[a] - lax.dot_general(
                rows[j, :, at_k], cols[core, xs * 4 + zs, :, at_k], (((1,), (1,)), ((), ())), preferred_element_type=jnp.float32
            )

    def batch(count, offsets, fresh):
        @pl.loop(0, 2 * count)
        def _(i):
            e, other = i // 2, i % 2
            dx, dz = offsets(e)

            @pl.when((other == 1) & (e >= fresh))
            def _():
                take_swap(at(dx, dz))

            multiply(dx, dz, other)

    barrier = pltpu.get_barrier_semaphore()
    near = [along_p(1), along_p(3), along_s(1), along_s(3), along_y(1), along_y(-1), partner]
    for to in near:
        pl.semaphore_signal(barrier, inc=1, device_id=to, device_id_type=MESH)
    pl.semaphore_wait(barrier, len(near))

    here = slot(0, 0)
    start(0, 1, 4, 5)
    swap(here, mine).start()
    row_start(0)
    own = pltpu.make_async_copy(mine, block(c, here), l_sem.at[4])
    own.start()
    for a in range(8):
        front(a).start()

    take_swap(here)
    row_start(1)
    row_forward(0)

    take(0, 1)
    start(2, 3)
    take(4, 5)
    start(6, 7, 8, 9, 12, 13)
    for p, s in ((3, 0), (1, 0), (0, 3), (0, 1)):
        swap(slot(p, s)).start()
    row_start(2)
    row_forward(1)
    take_swap(at(1, 0))
    take_swap(at(3, 0))
    row_start(3)

    take(2, 3)
    start(16, 17)
    swap(slot(2, 0)).start()
    take(6, 7)
    swap(slot(0, 2)).start()
    row_forward(2)

    take(8, 9)
    start(10, 11)
    swap(slot(3, 3)).start()
    swap(slot(3, 1)).start()
    row_forward(3)
    own.wait()
    for a in range(8):
        front(a).wait()
    row_take(0)
    row_take(1)
    batch(5, lambda e: (jnp.where(e == 1, 2, 0), jnp.where(e >= 2, e - 1, 0)), 1)

    take(12, 13)
    start(14, 15)
    swap(slot(1, 3)).start()
    swap(slot(1, 1)).start()
    row_take(2)
    row_take(3)
    batch(6, lambda e: (1 + 2 * (e % 2), ((e // 2) * (e // 2 + 1)) // 2), 2)

    take(16, 17)
    start(18, 19)
    swap(slot(2, 3)).start()
    swap(slot(2, 1)).start()
    pair, other_pair = x // 2, 1 - x // 2
    early = [pair * 4 + z, pair * 4 + (z + 1) % 4, pair * 4 + (z + 3) % 4, other_pair * 4 + z]
    late = [pair * 4 + (z + 2) % 4] + [other_pair * 4 + (z + d) % 4 for d in (1, 2, 3)]
    for a in early:
        result(a).start()

    def across(p, s, other):
        turn = c + other * (1 - 2 * c)
        return (1 - turn) * p + turn * s, turn * p + (1 - turn) * s

    @pl.loop(0, 4)
    def _(i):
        e, other = i // 2, i % 2
        dx, dz = across(2, 1 + 2 * e, other)

        @pl.when(other == 1)
        def _():
            take_swap(at(dx, dz))

        multiply(dx, dz, other)

    for q in (1, 2, 3):
        k = 4 + 4 * q
        take(k + 2, k + 3)
        swap(slot(Q_AT[q], 2)).start()

        @pl.loop(0, 2)
        def _(other):
            dx, dz = across(Q_AT[q], 2, other)

            @pl.when(other == 1)
            def _():
                take_swap(at(dx, dz))

            multiply(dx, dz, other)

    for a in late:
        result(a).start()
    for k in range(20):
        copy(k).wait_send()

    @pl.loop(0, 16)
    def _(at_slot):
        swap(at_slot).wait_send()

    for j in range(4):

        @pl.when(place == 0)
        def _():
            row_copy(j, 1).wait_send()
            row_copy(j, -1).wait_send()

        @pl.when(place == 1)
        def _():
            row_relay(j).wait_send()

    for a in early + late:
        result(a).wait()


def update(panels, front, wide, number):
    call = pl.pallas_call(
        functools.partial(kernel, wide),
        out_shape=jax.ShapeDtypeStruct(front.shape, jnp.float32),
        in_specs=[pl.BlockSpec(memory_space=pl.ANY)] * 2,
        out_specs=pl.BlockSpec(memory_space=pl.ANY),
        scratch_shapes=[
            pltpu.VMEM((2, 16, PIECE, wide), jnp.bfloat16),
            pltpu.VMEM((4, PIECE, wide), jnp.bfloat16),
            pltpu.VMEM((8, PIECE, PIECE), jnp.float32),
            pltpu.SemaphoreType.DMA((20,)),
            pltpu.SemaphoreType.DMA((20,)),
            pltpu.SemaphoreType.DMA((16,)),
            pltpu.SemaphoreType.DMA((16,)),
            pltpu.SemaphoreType.DMA((4, 2)),
            pltpu.SemaphoreType.DMA((4,)),
            pltpu.SemaphoreType.DMA((5,)),
            pltpu.SemaphoreType.DMA((8,)),
            pltpu.SemaphoreType.DMA((8,)),
        ],
        compiler_params=pltpu.CompilerParams(
            collective_id=number, has_side_effects=True, vmem_limit_bytes=67043328
        ),
    )
    return call(panels, front)


def shards(panels, sizes, front):
    count = panels.shape[1] // WIDTH
    limits = lax.dynamic_slice_in_dim(sizes, lax.axis_index("gz") * count, count, 0)
    column = jnp.arange(WIDTH, dtype=jnp.int32)
    live = (column[None, :] < limits[:, None]).reshape(count * WIDTH).astype(jnp.bfloat16)
    return update(panels * live[None, :], front, count * WIDTH, 0)


def solution(mesh):
    placed = (P(("gx", "gy"), "gz"), P(), P(("gx", "gz"), "gy"))
    return jax.shard_map(
        shards, mesh=mesh, in_specs=placed, out_specs=P(("gx", "gz"), "gy"), check_vma=False
    )
```

time: 415 us -> 152 us (0.37)
  waiting for transfers between devices: 362 us -> 0 us
  Pallas kernels: 0 us -> 143 us
  matrix products: 24.8 us -> 0 us
  between operations: 13.1 us -> 0.01 us
  other arithmetic: 7.05 us -> 2.73 us
    all_gather x2 -> x0, waiting for transfers between devices: 216 us -> none  [the longest x1 147 us: shards(): column_part = lax.all_gather(panels, 'gx', axis=0, tiled=True)]
    reduce_scatter x2 -> x0, waiting for transfers between devices: 145 us -> none  [sum_in_order(): blocks = lax.psum_scatter(blocks, axes[k], scatter_dimension=0, tiled=True)]
    pallas_call x0 -> x1, Pallas kernels: none -> 143 us  [update(): return call(panels, front)]
    dot_general x1 -> x0, matrix products: 24.8 us -> none  [shards(): lax.dot_general(masked, column_part, (((1,), (1,)), ((), ())), preferred_...]
    add x1 -> x0, other arithmetic: 6.98 us -> none  [shards(): return front + summed]
    transpose x1 -> x0, local copies, waits for them, and re-layouts: 6.81 us -> none  [sum_in_order(): jnp.moveaxis(blocks, sequence, range(len(axes))).reshape(-1, *inside)]
    unnamed x1 -> x2, local copies, waits for them, and re-layouts: 0.01 us -> 5.06 us
  transfers between devices with their start and end apart: 4 -> 0, of which waited for: 4 -> 0; matrix products, arithmetic and copies ran while one was open for 0% -> 0% of each run, Pallas kernels for 0% -> 0%
where the time goes in v1:
time: 152 us; the launch traced here: 151 us
  Pallas kernels  143 us (94%)
  local copies, waits for them, and re-layouts  5.79 us (4%)
  other arithmetic  2.73 us (2%)
    pallas_call x1, Pallas kernels, update(): return call(panels, front)  143 us
    unnamed x2, local copies, waits for them, and re-layouts  5.06 us

profile of v1, /device:TPU:1, one launch (start us, length us, event | category | flops | bytes accessed | tf_op | source)
XLA Modules:
  0.0 151.1 jit_solution(6440066975789758204)
XLA Ops:
  0.0 0.7 dynamic_slice.3
  0.7 0.1 fusion
  0.8 2.7 %broadcast_multiply_fusion.p_ref = bf16[384,2048]{1,0:T(8,128)(2,1)} fusion(bf16[384,2048]{1,0:T(8,128)(2,1)} %param.3, bf16[2048]{0:T(1024)(128)(2,1)S(1)} %bitcast.5), kind=kLoop, calls=%fused_computation | loop fusion | flops 786432 | bytes 3149824 | tf_op jit(solution)/shard_map/mul | solution.py:325
  3.5 142.6 %shard_map.37 = f32[384,3072]{1,0:T(8,128)} custom-call(bf16[384,2048]{1,0:T(8,128)(2,1)} %broadcast_multiply_fusion.p_ref, f32[384,3072]{1,0:T(8,128)} %f_ref.1), custom_call_target="tpu_custom_call" | custom-call | tf_op jit(solution)/shard_map/pallas_call | solution.py:317
  146.1 5.1 %copy.8 = f32[384,3072]{1,0:T(8,128)} copy(f32[384,3072]{1,0:T(8,128)} %shard_map.37) | data formatting | bytes 9437184
  (1 shorter events, 0.0 us)

commit v2 on v1

--- a/solution.py
+++ b/solution.py
@@ -10,16 +10,18 @@
 WIDTH = 1024
 PIECE = 384
 HALF = PIECE // 2
-CHUNK = 512
+LANES = 128
+ROWS = 32
 MESH = pl.DeviceIdType.MESH
 Q_AT = (0, 3, 1, 2)
+WIDES = (768, 896, 1024, 1152, 1280, 1408, 1536, 1664, 1792, 2048)
 
 
 def device(x, y, z, c):
     return (x // 2) * 4 + z, y, (x % 2) * 2 + c
 
 
-def kernel(wide, p_ref, f_ref, o_ref, cols, rows, acc, s_send, s_recv, x_send, x_recv, y_send, y_recv, l_sem, f_sem, o_sem):
+def kernel(wide, p_ref, f_ref, o_ref, stage, cols, rows, acc, r_send, r_recv, s_send, s_recv, x_send, x_recv, y_send, y_recv, l_sem, f_sem, o_sem):
     gx, y, gz = lax.axis_index("gx"), lax.axis_index("gy"), lax.axis_index("gz")
     x_lo, c, z = gz // 2, gz % 2, gx % 4
     x = (gx // 4) * 2 + x_lo
@@ -41,7 +43,6 @@
         return device(x, (y + 4 + d * sign) % 4, z, c)
 
     partner = device(x, y, z, 1 - c)
-    mine = p_ref.at[:, pl.ds(0, wide)]
     whole, top, bottom = pl.ds(0, PIECE), pl.ds(0, HALF), pl.ds(HALF, HALF)
 
     def block(core, at_slot, part=whole):
@@ -52,14 +53,14 @@
 
     def copy(k):
         if k < 2:
-            return send(k, mine, block(c, slot(0, 0)), along_p(1 + 2 * k))
+            return send(k, block(c, slot(0, 0)), block(c, slot(0, 0)), along_p(1 + 2 * k))
         if k < 4:
             ref = block(c, slot(3 if k == 2 else 1, 0), (top, bottom)[k - 2])
             return send(k, ref, ref, along_p(2 * k - 3))
         q, kind = k // 4 - 1, k % 4
         if kind < 2:
             here = block(c, slot(Q_AT[q], 0))
-            return send(k, mine if q == 0 else here, here, along_s(1 + 2 * kind))
+            return send(k, here, here, along_s(1 + 2 * kind))
         ref = block(c, slot(Q_AT[q], 3 if kind == 2 else 1), (top, bottom)[kind - 2])
         return send(k, ref, ref, along_s(2 * kind - 3))
 
@@ -81,8 +82,8 @@
         for k in ks:
             arrival(k).wait_recv()
 
-    def swap(at_slot, src=None):
-        src = block(c, at_slot) if src is None else src
+    def swap(at_slot):
+        src = block(c, at_slot)
         return pltpu.make_async_remote_copy(
             src, block(c, at_slot), x_send.at[at_slot], x_recv.at[at_slot], device_id=partner, device_id_type=MESH
         )
@@ -97,8 +98,6 @@
     beside = x + 1 - 2 * x_lo
 
     def row_src(j):
-        if j == 0:
-            return mine
         return block(c if j % 2 == 0 else 1 - c, (beside if j >= 2 else x) * 4 + z)
 
     def row_copy(j, d):
@@ -149,39 +148,42 @@
         core = c + other * (1 - 2 * c)
         j = 2 * (dx % 2) + other
 
-        @pl.loop(0, wide // CHUNK)
-        def _(i):
-            at_k = pl.ds(pl.multiple_of(i * CHUNK, CHUNK), CHUNK)
-            acc[a] = acc[a] - lax.dot_general(
-                rows[j, :, at_k], cols[core, xs * 4 + zs, :, at_k], (((1,), (1,)), ((), ())), preferred_element_type=jnp.float32
-            )
-
-    def batch(count, offsets, fresh):
-        @pl.loop(0, 2 * count)
-        def _(i):
-            e, other = i // 2, i % 2
-            dx, dz = offsets(e)
-
-            @pl.when((other == 1) & (e >= fresh))
-            def _():
-                take_swap(at(dx, dz))
-
-            multiply(dx, dz, other)
-
+        acc[a] = acc[a] - lax.dot_general(
+            rows[j], cols[core, xs * 4 + zs], (((1,), (1,)), ((), ())), preferred_element_type=jnp.float32
+        )
+
+    here = slot(0, 0)
+
+    own = pltpu.make_async_copy(p_ref.at[:, pl.ds(pl.multiple_of(c * wide, LANES), wide)], block(c, here), l_sem.at[4])
+    own.start()
+    for a in range(8):
+        front(a).start()
     barrier = pltpu.get_barrier_semaphore()
     near = [along_p(1), along_p(3), along_s(1), along_s(3), along_y(1), along_y(-1), partner]
     for to in near:
         pl.semaphore_signal(barrier, inc=1, device_id=to, device_id_type=MESH)
     pl.semaphore_wait(barrier, len(near))
 
-    here = slot(0, 0)
+    share = pltpu.make_async_remote_copy(
+        p_ref.at[:, pl.ds(pl.multiple_of((1 - c) * wide, LANES), wide)],
+        stage,
+        r_send,
+        r_recv,
+        device_id=partner,
+        device_id_type=MESH,
+    )
+    share.start()
+    own.wait()
+    share.wait_recv()
+
+    @pl.loop(0, PIECE // ROWS)
+    def _(i):
+        at_rows = pl.ds(pl.multiple_of(i * ROWS, ROWS), ROWS)
+        cols[c, here, at_rows] = cols[c, here, at_rows] + stage[at_rows]
+
     start(0, 1, 4, 5)
-    swap(here, mine).start()
+    swap(here).start()
     row_start(0)
-    own = pltpu.make_async_copy(mine, block(c, here), l_sem.at[4])
-    own.start()
-    for a in range(8):
-        front(a).start()
 
     take_swap(here)
     row_start(1)
@@ -211,63 +213,61 @@
     swap(slot(3, 3)).start()
     swap(slot(3, 1)).start()
     row_forward(3)
-    own.wait()
     for a in range(8):
         front(a).wait()
     row_take(0)
     row_take(1)
-    batch(5, lambda e: (jnp.where(e == 1, 2, 0), jnp.where(e >= 2, e - 1, 0)), 1)
-
-    take(12, 13)
-    start(14, 15)
-    swap(slot(1, 3)).start()
-    swap(slot(1, 1)).start()
-    row_take(2)
-    row_take(3)
-    batch(6, lambda e: (1 + 2 * (e % 2), ((e // 2) * (e // 2 + 1)) // 2), 2)
-
-    take(16, 17)
-    start(18, 19)
-    swap(slot(2, 3)).start()
-    swap(slot(2, 1)).start()
     pair, other_pair = x // 2, 1 - x // 2
     early = [pair * 4 + z, pair * 4 + (z + 1) % 4, pair * 4 + (z + 3) % 4, other_pair * 4 + z]
     late = [pair * 4 + (z + 2) % 4] + [other_pair * 4 + (z + d) % 4 for d in (1, 2, 3)]
-    for a in early:
-        result(a).start()
-
-    def across(p, s, other):
+
+    @pl.loop(0, 32)
+    def _(i):
+        @pl.when(i == 10)
+        def _():
+            take(12, 13)
+            start(14, 15)
+            swap(slot(1, 3)).start()
+            swap(slot(1, 1)).start()
+            row_take(2)
+            row_take(3)
+
+        @pl.when(i == 22)
+        def _():
+            take(16, 17)
+            start(18, 19)
+            swap(slot(2, 3)).start()
+            swap(slot(2, 1)).start()
+            for a in early:
+                result(a).start()
+
+        for q in (1, 2, 3):
+
+            @pl.when(i == 24 + 2 * q)
+            def _():
+                take(6 + 4 * q, 7 + 4 * q)
+                swap(slot(Q_AT[q], 2)).start()
+
+        other = i % 2
+        e, f, g, h = i // 2, i // 2 - 5, i // 2 - 11, i // 2 - 13
+        ahead = jnp.where(i < 26, 2, jnp.where(h == 0, 3, h))
+        aside = jnp.where(i < 26, 1 + 2 * g, 2)
         turn = c + other * (1 - 2 * c)
-        return (1 - turn) * p + turn * s, turn * p + (1 - turn) * s
-
-    @pl.loop(0, 4)
-    def _(i):
-        e, other = i // 2, i % 2
-        dx, dz = across(2, 1 + 2 * e, other)
-
-        @pl.when(other == 1)
+        late_x, late_z = (1 - turn) * ahead + turn * aside, turn * ahead + (1 - turn) * aside
+        near_x, near_z = jnp.where(e == 1, 2, 0), jnp.where(e >= 2, e - 1, 0)
+        next_x, next_z = 1 + 2 * (f % 2), (f // 2) * (f // 2 + 1) // 2
+        dx = jnp.where(i < 10, near_x, jnp.where(i < 22, next_x, late_x))
+        dz = jnp.where(i < 10, near_z, jnp.where(i < 22, next_z, late_z))
+
+        @pl.when((other == 1) & (i != 1) & (i != 11) & (i != 13))
         def _():
             take_swap(at(dx, dz))
 
         multiply(dx, dz, other)
-
-    for q in (1, 2, 3):
-        k = 4 + 4 * q
-        take(k + 2, k + 3)
-        swap(slot(Q_AT[q], 2)).start()
-
-        @pl.loop(0, 2)
-        def _(other):
-            dx, dz = across(Q_AT[q], 2, other)
-
-            @pl.when(other == 1)
-            def _():
-                take_swap(at(dx, dz))
-
-            multiply(dx, dz, other)
 
     for a in late:
         result(a).start()
+    share.wait_send()
     for k in range(20):
         copy(k).wait_send()
 
@@ -290,16 +290,56 @@
         result(a).wait()
 
 
-def update(panels, front, wide, number):
+def pack(sizes_ref, p_ref, o_ref, branch_ref):
+    gz = lax.axis_index("gz")
+    totals = [sum(sizes_ref[4 * k + i] for i in range(4)) for k in range(2)]
+    need = (jnp.maximum(totals[0], totals[1]) + 1) // 2
+    branch, wide = 0, WIDES[0]
+    for low, high in zip(WIDES[:-1], WIDES[1:]):
+        over = (need > low).astype(jnp.int32)
+        branch, wide = branch + over, wide + over * (high - low)
+    branch_ref[0] = branch
+    sizes = [sizes_ref[2 * gz], sizes_ref[2 * gz + 1]]
+    begin = (gz % 2) * (2 * wide - sizes[0] - sizes[1])
+    begins = [begin, begin + sizes[0], begin + sizes[0] + sizes[1]]
+    shift = lax.broadcasted_iota(jnp.int32, (2 * LANES, LANES), 0) - lax.broadcasted_iota(jnp.int32, (2 * LANES, LANES), 1)
+    lane = lax.broadcasted_iota(jnp.int32, (2 * LANES, LANES), 1)
+
+    @pl.loop(0, 2 * wide // LANES)
+    def _(t):
+        first = t * LANES
+        here = pl.ds(pl.multiple_of(first, LANES), LANES)
+        used = (first < begins[2]) & (first + LANES > begins[0])
+
+        @pl.when(used)
+        def _():
+            total = jnp.zeros((PIECE, LANES), jnp.float32)
+            for k in range(2):
+                ahead = first - begins[k]
+                window = jnp.clip((ahead + 4 * WIDTH) // LANES * LANES - 4 * WIDTH, 0, WIDTH - 2 * LANES)
+                pick = (shift == ahead - window) & (lane < begins[k + 1] - first)
+                part = p_ref[:, pl.ds(pl.multiple_of(k * WIDTH + window, LANES), 2 * LANES)]
+                total += jnp.dot(part, pick.astype(jnp.bfloat16), preferred_element_type=jnp.float32)
+            o_ref[:, here] = total.astype(jnp.bfloat16)
+
+        @pl.when(jnp.logical_not(used))
+        def _():
+            o_ref[:, here] = jnp.zeros((PIECE, LANES), jnp.bfloat16)
+
+
+def update(wide, number, packed, front):
     call = pl.pallas_call(
         functools.partial(kernel, wide),
         out_shape=jax.ShapeDtypeStruct(front.shape, jnp.float32),
         in_specs=[pl.BlockSpec(memory_space=pl.ANY)] * 2,
         out_specs=pl.BlockSpec(memory_space=pl.ANY),
         scratch_shapes=[
+            pltpu.VMEM((PIECE, wide), jnp.bfloat16),
             pltpu.VMEM((2, 16, PIECE, wide), jnp.bfloat16),
             pltpu.VMEM((4, PIECE, wide), jnp.bfloat16),
             pltpu.VMEM((8, PIECE, PIECE), jnp.float32),
+            pltpu.SemaphoreType.DMA,
+            pltpu.SemaphoreType.DMA,
             pltpu.SemaphoreType.DMA((20,)),
             pltpu.SemaphoreType.DMA((20,)),
             pltpu.SemaphoreType.DMA((16,)),
@@ -314,15 +354,21 @@
             collective_id=number, has_side_effects=True, vmem_limit_bytes=67043328
         ),
     )
-    return call(panels, front)
+    return call(packed, front)
 
 
 def shards(panels, sizes, front):
-    count = panels.shape[1] // WIDTH
-    limits = lax.dynamic_slice_in_dim(sizes, lax.axis_index("gz") * count, count, 0)
-    column = jnp.arange(WIDTH, dtype=jnp.int32)
-    live = (column[None, :] < limits[:, None]).reshape(count * WIDTH).astype(jnp.bfloat16)
-    return update(panels * live[None, :], front, count * WIDTH, 0)
+    packed, branch = pl.pallas_call(
+        pack,
+        out_shape=[
+            jax.ShapeDtypeStruct((PIECE, 4 * WIDTH), jnp.bfloat16),
+            jax.ShapeDtypeStruct((1,), jnp.int32),
+        ],
+        in_specs=[pl.BlockSpec(memory_space=pltpu.SMEM), pl.BlockSpec(memory_space=pltpu.VMEM)],
+        out_specs=[pl.BlockSpec(memory_space=pltpu.VMEM), pl.BlockSpec(memory_space=pltpu.SMEM)],
+    )(sizes, panels)
+    calls = [functools.partial(update, wide, number) for number, wide in enumerate(WIDES)]
+    return lax.switch(branch[0], calls, packed, front)
 
 
 def solution(mesh):

time: 152 us -> 101 us (0.66)
  Pallas kernels: 143 us -> 94.1 us
  other arithmetic: 2.73 us -> 0 us
    pallas_call x1 -> x2, Pallas kernels: 143 us -> 94.1 us  [the longest x1 87.9 us: update(): return call(packed, front)]
    mul x1 -> x0, other arithmetic: 2.66 us -> none  [shards(): return update(panels * live[None, :], front, count * WIDTH, 0)]
    unnamed x2 -> x1, local copies, waits for them, and re-layouts: 5.06 us -> 5.05 us
where the time goes in v2:
time: 101 us; the launch traced here: 100 us
  Pallas kernels  94.1 us (93%)
  local copies, waits for them, and re-layouts  5.05 us (5%)
    pallas_call x1, Pallas kernels, update(): return call(packed, front)  87.9 us
    pallas_call x1, Pallas kernels, shards(): pl.pallas_call(pack, out_shape=[jax.ShapeDtypeStruct((PIECE, 4 * WIDTH),...  6.2 us
    unnamed x1, local copies, waits for them, and re-layouts  5.05 us

profile of v2, /device:TPU:1, one launch (start us, length us, event | category | flops | bytes accessed | tf_op | source)
XLA Modules:
  0.0 100.0 jit_solution(16621418146405867612)
XLA Ops:
  0.0 6.2 %shard_map.47 = (bf16[384,4096]{1,0:T(8,128)(2,1)}, s32[1]{0:T(128)}) custom-call(s32[8]{0:T(128)} %sizes_ref.1, bf16[384,2048]{1,0:T(8,128)(2,1)} %p_ref.1), custom_call_target="tpu_custom_call" | custom-call | tf_op jit(solution)/shard_map/pallas_call | solution.py:361
  6.8 88.1 %conditional.1 = (f32[384,3072]{1,0:T(8,128)}) conditional(s32[]{:T(128)} %bitcast, (bf16[384,4096]{1,0:T(8,128)(2,1)}, f32[384,3072]{1,0:T(8,128)}) %tuple.35, (bf16[384,4096]{1,0:T(8,128)(2,1)}, f32[384,3072]{1,0:T(8,128)}) %tuple.35, (bf16[384,4096]{1,0:T(8,128)(2,1)}, f32[384,3072]{1,0:T(8,128)}) %tuple.35, ...), branch_computations={%region_0.0_spmd, %region_1.0_spmd, %region_2.0_spmd, %region_3.0_... | conditional | bytes 8 | solution.py:371
  6.9 87.9 %branch_3_fun.1 = f32[384,3072]{1,0:T(8,128)} custom-call(bf16[384,4096]{1,0:T(8,128)(2,1)} %get-tuple-element.60.p_ref, f32[384,3072]{1,0:T(8,128)} %get-tuple-element.62.f_ref), custom_call_target="tpu_custom_call" | custom-call | tf_op jit(solution)/shard_map/cond/branch_3_fun/pallas_call | solution.py:357
  95.0 5.1 %copy.25 = f32[384,3072]{1,0:T(8,128)} copy(f32[384,3072]{1,0:T(8,128)} %get-tuple-element.80) | data formatting | bytes 9437184
